TPU v7x, 32 devices: a whole 2x2x4 slice. The times are simulated.
32 devices in a mesh: mem: 4 (over z), gx: 4 (over y, core), gy: 2 (over x).
Axes of the slice: x: 2, y: 2, z: 4, core: 2. Of those that a mesh axis runs over, the one named last changes fastest.
Arguments:
- height: float32 [4, 4, 128, 256], P('mem', None, 'gx', 'gy'), may hold values from -4 to 4
- wind: float32 [4, 2, 4, 128, 256], P('mem', None, None, 'gx', 'gy'), may hold values from -0.8 to 0.8
- moisture: float32 [4, 4, 128, 256], P('mem', None, 'gx', 'gy'), may hold values from 0 to 2
- coeffs: float32 [4, 4, 4, 16384], P('mem', None, None, ('gx', 'gy')), may hold values from -6 to 6
- damping: float32 [16384], P(('gx', 'gy')), may hold values from 0.3 to 1
- vmix: float32 [4, 4], replicated, may hold values from -3 to 3
- basis: bfloat16 [16384, 384], P(('gx', 'gy')), may hold values from -0.046875 to 0.046875
- edge_source: int32 [768], replicated, may hold values from 0 to 383
- row_cell: int32 [128], replicated, may hold values from 0 to 15, never falling along the last dimension, each value on 1 to 16 neighbouring positions
- col_cell: int32 [256], replicated, may hold values from 0 to 31, never falling along the last dimension, each value on 1 to 16 neighbouring positions
- cond_rate: float32 [4], replicated, may hold values from 0.05 to 0.5
- saturation: float32 [4], replicated, may hold values from 0.5 to 1.5
- ancestry: int32 [4], replicated, may hold values from 0 to 3
Outputs:
- height_out: float32 [4, 4, 128, 256], P('mem', None, 'gx', 'gy')
- wind_out: float32 [4, 2, 4, 128, 256], P('mem', None, None, 'gx', 'gy')
- moisture_out: float32 [4, 4, 128, 256], P('mem', None, 'gx', 'gy')
- rainfall: float32 [4, 128, 256], P('mem', 'gx', 'gy')
- restricted: float32 [4, 4, 16, 32], P('mem')
- coeffs_out: float32 [4, 4, 4, 16384], P('mem', None, None, ('gx', 'gy'))
Inputs may be any that keep to these rules, and one draw needn't show every extreme that they name: row_cell never falls, and each of the 16 global rows holds 1 to 16 nest rows, one exactly 16. col_cell never falls, and each of the 32 global columns holds 1 to 16 nest columns, one exactly 16.
All inputs are finite; a program needn't handle non-finite values.
Results may differ from a plain program's by a relative error of at most 0.00035.
Values sent between devices are 32-bit elements; how exact they have to be, the bound alone decides.
A program may use at most 64 MiB of HBM per device.

v0:
```python
import functools

import jax
import jax.numpy as jnp
from jax import lax
from jax.experimental import pallas as pl
from jax.experimental.pallas import tpu as pltpu
from jax.sharding import PartitionSpec as P

RATIO = 8
ACOUSTIC = 2
HALO = 8
SPLIT = 3

acoustic_substep = 0.2
drift_step = 0.4

MESH = pl.DeviceIdType.MESH


def kernel(
    sizes,
    height,
    wind,
    moisture,
    coeffs_hbm,
    damping_hbm,
    vmix_hbm,
    basis_hbm,
    edge_source_hbm,
    row_cell_hbm,
    col_cell_hbm,
    cond_rate_hbm,
    saturation_hbm,
    ancestry_hbm,
    height_out,
    wind_out,
    moisture_out,
    rain_out,
    coarse_out,
    coeffs_out,
    coeffs,
    damping,
    vmix,
    basis,
    edge_source,
    row_cell,
    col_cell,
    cond_rate,
    saturation,
    ancestry,
    st,
    cf,
    st_sel,
    cf_sel,
    st_relay,
    cur,
    rows_out,
    rows_in,
    packed,
    packed_in,
    diag_in,
    rim_part,
    rim_in,
    rim_z,
    rim_full,
    table,
    sides,
    sides_t,
    coarse_rows_buf,
    coarse_part,
    coarse_in,
    halo_send,
    halo_recv,
    rim_send,
    rim_recv,
    rimz_send,
    rimz_recv,
    rimg_send,
    rimg_recv,
    crs_send,
    crs_recv,
    mem_send,
    mem_recv,
    local,
):
    members, count_x, count_y = sizes
    plane = count_x * count_y
    levels = st.shape[1]
    size_x = st.shape[3]
    size_y = st.shape[4]
    full_x = row_cell.shape[1]
    full_y = col_cell.shape[1]
    rim_points = basis.shape[1]
    coarse_x = coarse_out.shape[2]
    coarse_y = coarse_out.shape[3]
    share = rim_part.shape[1]
    f32 = jnp.float32

    z = lax.axis_index("mem")
    ix = lax.axis_index("gx")
    iy = lax.axis_index("gy")
    here = ix * count_y + iy
    low_side = z < 2
    inner = jnp.logical_and(z > 0, z < members - 1)
    outer = jnp.logical_not(inner)
    near = jnp.where(low_side, 1 - z, 5 - z)
    cross_inner = jnp.where(low_side, 2, 1)
    cross_outer = jnp.where(low_side, 3, 0)

    def plane_peer(step):
        other = lax.rem(here + step, plane)
        return other, other // count_y, lax.rem(other, count_y)

    loads = [
        (coeffs_hbm, coeffs),
        (damping_hbm, damping),
        (vmix_hbm, vmix),
        (height.at[0], st.at[z, :, 0]),
        (wind.at[0, 0], st.at[z, :, 1]),
        (wind.at[0, 1], st.at[z, :, 2]),
        (moisture.at[0], st.at[z, :, 3]),
        (basis_hbm, basis),
        (edge_source_hbm, edge_source),
        (row_cell_hbm, row_cell),
        (col_cell_hbm, col_cell),
        (cond_rate_hbm, cond_rate),
        (saturation_hbm, saturation),
        (ancestry_hbm, ancestry),
    ]
    copies = [pltpu.make_async_copy(a, b, local.at[n]) for n, (a, b) in enumerate(loads)]
    for copy in copies:
        copy.start()

    def ready(*which):
        for n in which:
            copies[n].wait()

    barrier = pltpu.get_barrier_semaphore()
    for step in range(1, plane):
        _, px, py = plane_peer(step)
        pl.semaphore_signal(barrier, inc=1, device_id=(z, px, py), device_id_type=MESH)
    for step in range(1, members):
        pl.semaphore_signal(
            barrier,
            inc=1,
            device_id=(lax.rem(z + step, members), ix, iy),
            device_id_type=MESH,
        )

    ready(0, 1, 2)
    new_fields = []
    for f in range(4):
        c = coeffs[0, f]
        acc = vmix[:, 0:1] * c[0:1]
        for j in range(1, levels):
            acc = acc + vmix[:, j : j + 1] * c[j : j + 1]
        new_fields.append(acc * damping[...])
    for f in range(4):
        cf[z, f // 2, f % 2] = new_fields[f]
    ready(3, 4, 5, 6)

    pl.semaphore_wait(barrier, plane - 1 + members - 1)

    def chunk(c, slot):
        return st.at[slot, c] if c < levels else cf.at[slot, c - levels]

    def chosen(c, way):
        return st_sel.at[way, c] if c < levels else cf_sel.at[way, c - levels]

    def z_copy(c, kind, src, slot, target, way):
        return pltpu.make_async_remote_copy(
            src_ref=src,
            dst_ref=chunk(c, slot),
            send_sem=mem_send.at[c, way],
            recv_sem=mem_recv.at[c, kind],
            device_id=(target, ix, iy),
            device_id_type=MESH,
        )

    def own_near(c):
        return z_copy(c, 0, chunk(c, z), z, near, 0)

    def own_cross(c):
        return z_copy(c, jnp.where(outer, 2, 1), chunk(c, z), z, cross_inner, 1)

    def sel_inner(c):
        return z_copy(c, 1, chosen(c, 0), z, cross_inner, 1)

    def sel_outer(c):
        return z_copy(c, 1, chosen(c, 1), z, cross_outer, 2)

    def relay_near(c):
        return z_copy(c, 0, st_relay, z, near, 0)

    def arrived(c, kind, slot):
        z_copy(c, kind, chunk(c, slot), slot, near, 0).wait_recv()

    first, rest = 0, list(range(1, levels))
    specs = [levels, levels + 1]

    @pl.when(inner)
    def _():
        own_cross(first).start()
        for c in rest:
            own_near(c).start()

    @pl.when(outer)
    def _():
        own_near(rest[0]).start()
        own_cross(first).start()
        for c in rest[1:] + [first] + specs:
            own_near(c).start()

    low = jnp.concatenate(new_fields, axis=0).astype(jnp.bfloat16)
    ready(7)
    part = jnp.dot(low, basis[...], preferred_element_type=f32)
    for g in range(count_x):
        rim_part[g] = part[g * share : (g + 1) * share]

    def rim_copy(step):
        _, px, py = plane_peer(step)
        return pltpu.make_async_remote_copy(
            src_ref=rim_part.at[px],
            dst_ref=rim_in.at[here],
            send_sem=rim_send.at[step],
            recv_sem=rim_recv.at[here],
            device_id=(z, px, py),
            device_id_type=MESH,
        )

    for step in range(1, plane):
        rim_copy(step).start()

    ready(8, 9, 10, 11, 12, 13)
    mine = ancestry[z]

    def select_near(c):
        arrived(c, 0, near)
        for way, target in ((0, cross_inner), (1, cross_outer)):
            take_own = ancestry[target] != near
            chosen(c, way)[...] = jnp.where(take_own, chunk(c, z)[...], chunk(c, near)[...])

    @pl.when(inner)
    def _():
        c = rest[0]
        select_near(c)
        sel_outer(c).start()
        sel_inner(c).start()

    n_edge = edge_source.shape[0]
    table[...] = (
        (lax.broadcasted_iota(jnp.int32, (rim_points, n_edge), 0)
         == edge_source[...].reshape(1, n_edge))
        .astype(f32)
        .astype(jnp.bfloat16)
    )
    row_table = (
        lax.broadcasted_iota(jnp.int32, (coarse_x, full_x), 0) == row_cell[...]
    ).astype(f32)
    row_count = jnp.sum(row_table, axis=1, keepdims=True)
    wide = lax.rem(
        lax.broadcasted_iota(jnp.int32, (levels * coarse_y, full_y), 0), coarse_y
    )
    col_table = (wide == col_cell[...]).astype(f32)
    col_count = lax.dot_general(
        jnp.ones((8, full_y), f32),
        col_table,
        (((1,), (1,)), ((), ())),
        preferred_element_type=f32,
    )[0:1]
    col_off = pl.multiple_of(iy * size_y, 128)
    row_off = pl.multiple_of(ix * size_x, 8)
    cells_here = col_cell[:, pl.ds(col_off, size_y)]
    wide_here = lax.broadcasted_iota(jnp.int32, (levels * coarse_y, size_y), 0)
    coarse_rows_buf[...] = jnp.zeros_like(coarse_rows_buf)

    total = rim_part[ix]
    for step in range(1, plane):
        other, px, py = plane_peer(step)
        pltpu.make_async_remote_copy(
            src_ref=rim_part.at[px],
            dst_ref=rim_in.at[other],
            send_sem=rim_send.at[step],
            recv_sem=rim_recv.at[other],
            device_id=(z, px, py),
            device_id_type=MESH,
        ).wait_recv()
        total = total + rim_in[other]
    rim_z[z] = total

    def rimz_copy(step, source):
        return pltpu.make_async_remote_copy(
            src_ref=rim_z.at[source],
            dst_ref=rim_z.at[source],
            send_sem=rimz_send.at[step],
            recv_sem=rimz_recv.at[source],
            device_id=(lax.rem(z + step, members), ix, iy),
            device_id_type=MESH,
        )

    for step in range(1, members):
        rimz_copy(step, z).start()

    @pl.when(inner)
    def _():
        arrived(first, 1, cross_inner)
        arrived(first, 2, cross_outer)
        want = ancestry[near]
        a = st[z, first]
        a = jnp.where(want == cross_inner, st[cross_inner, first], a)
        st_relay[...] = jnp.where(want == cross_outer, st[cross_outer, first], a)
        relay_near(first).start()
        for c in specs:
            own_near(c).start()
        for c in rest[1:]:
            select_near(c)
            sel_outer(c).start()
        for c in rest[1:]:
            sel_inner(c).start()

    share_sel = rim_z[z]
    for step in range(1, members):
        source = lax.rem(z + step, members)
        rimz_copy(step, source).wait_recv()
        share_sel = jnp.where(mine == source, rim_z[source], share_sel)
    rim_full[ix] = share_sel

    def rimg_copy(step, source):
        return pltpu.make_async_remote_copy(
            src_ref=rim_full.at[source],
            dst_ref=rim_full.at[source],
            send_sem=rimg_send.at[step],
            recv_sem=rimg_recv.at[source],
            device_id=(z, lax.rem(ix + step, count_x), iy),
            device_id_type=MESH,
        )

    for step in range(1, count_x):
        rimg_copy(step, ix).start()

    lane = lax.broadcasted_iota(jnp.int32, (size_x, size_y), 1)
    width = size_y // (4 * levels)
    half = width // 2

    def settle(c, ref):
        arrived(c, 1, cross_inner)

        @pl.when(outer)
        def _():
            arrived(c, 0, near)

        a = jnp.where(mine == z, chunk(c, z)[...], chunk(c, cross_inner)[...])
        ref[...] = jnp.where(mine == near, chunk(c, near)[...], a)

    @pl.when(outer)
    def _():
        arrived(first, 0, near)
        cur[first] = jnp.where(mine == z, st[z, first], st[near, first])

    @pl.when(inner)
    def _():
        arrived(first, 0, near)
        a = jnp.where(mine == cross_inner, st[cross_inner, first], st[cross_outer, first])
        a = jnp.where(mine == near, st[near, first], a)
        cur[first] = jnp.where(mine == z, st[z, first], a)
        for c in specs:
            select_near(c)
            sel_outer(c).start()
        for c in specs:
            sel_inner(c).start()

    groups = [list(range(SPLIT)), list(range(SPLIT, levels))]

    def halo_jobs(g, mode):
        lo, n_lev = groups[g][0], len(groups[g])
        lev = pl.ds(lo, n_lev)
        for dx in (-1, 0, 1):
            for dy in (-1, 0, 1):
                if dx == 0 and dy == 0:
                    continue
                flip = -1 if mode == "recv" else 1
                ok = jnp.bool_(True)
                if dx * flip == -1:
                    ok = jnp.logical_and(ok, ix > 0)
                if dx * flip == 1:
                    ok = jnp.logical_and(ok, ix < count_x - 1)
                if dy * flip == -1:
                    ok = jnp.logical_and(ok, iy > 0)
                if dy * flip == 1:
                    ok = jnp.logical_and(ok, iy < count_y - 1)
                sx = 0 if dx == -1 else 1
                sy = 0 if dy == -1 else 1
                rows = pl.ds(0, HALO) if dx == -1 else pl.ds(size_x - HALO, HALO)
                if dy == 0:
                    src, dst, base = rows_out.at[sx, lev], rows_in.at[sx, lev], sx
                elif dx == 0:
                    src, dst, base = packed.at[g], packed_in.at[g, sy], 2 + sy
                else:
                    src, dst = packed.at[g, rows, :], diag_in.at[g, sx, sy]
                    base = 4 + 2 * sx + sy

                def go(src=src, dst=dst, base=base, target=(z, ix + dx, iy + dy)):
                    copy = pltpu.make_async_remote_copy(
                        src_ref=src,
                        dst_ref=dst,
                        send_sem=halo_send.at[g, base],
                        recv_sem=halo_recv.at[g, base],
                        device_id=target,
                        device_id_type=MESH,
                    )
                    if mode == "start":
                        copy.start()
                    elif mode == "send":
                        copy.wait_send()
                    else:
                        copy.wait_recv()

                pl.when(ok)(go)

    def halo_out(g):
        pack = jnp.zeros((size_x, size_y), f32)
        for l in groups[g]:
            if l != first:
                settle(l, cur.at[l])
            for f in range(4):
                rows_out[0, l, f] = cur[l, f, 0:HALO]
                rows_out[1, l, f] = cur[l, f, size_x - HALO :]
                k = f * levels + l
                moved = pltpu.roll(cur[l, f], (width * k + half) % size_y, 1)
                pack = jnp.where(lane // width == k, moved, pack)
        packed[g] = pack
        halo_jobs(g, "start")

    halo_out(0)
    halo_out(1)

    ext_x = size_x + 2 * HALO
    ext_y = 2 * size_y
    rpos = lax.broadcasted_iota(jnp.int32, (ext_x, ext_y), 0)
    cpos = lax.broadcasted_iota(jnp.int32, (ext_x, ext_y), 1)
    gx_pos = ix * size_x + jnp.where(rpos < size_x + HALO, rpos, rpos - ext_x)
    gy_pos = iy * size_y + jnp.where(cpos < size_y + size_y // 2, cpos, cpos - ext_y)
    inside = (gx_pos >= 0) & (gx_pos < full_x) & (gy_pos >= 0) & (gy_pos < full_y)
    at_west = gx_pos == -1
    at_east = gx_pos == full_x
    at_south = gy_pos == -1

    for step in range(1, count_x):
        rimg_copy(step, lax.rem(ix + step, count_x)).wait_recv()
    rim = jnp.concatenate([rim_full[g] for g in range(count_x)], axis=0)
    rim_hi = rim.astype(jnp.bfloat16)
    rim_lo = (rim - rim_hi.astype(f32)).astype(jnp.bfloat16)
    both = jnp.dot(
        jnp.concatenate([rim_hi, rim_lo], axis=0), table[...], preferred_element_type=f32
    )
    n_rows = 4 * levels
    edge = both[0:n_rows] + both[n_rows:]
    sides[...] = edge
    for s in range(2):
        begin = 2 * full_y + s * full_x
        sides_t[s, HALO : HALO + full_x, :] = edge[:, begin : begin + full_x].T
        sides_t[s, 0:HALO, :] = jnp.zeros((HALO, n_rows), f32)
        sides_t[s, HALO + full_x :, :] = jnp.zeros((HALO, n_rows), f32)
    lane1 = lax.broadcasted_iota(jnp.int32, (n_rows, size_y), 1)

    def x_side(begin):
        own = sides[:, pl.ds(pl.multiple_of(begin + col_off, 128), size_y)]
        after = lax.rem(iy + 1, count_y) * size_y
        before = lax.rem(iy + count_y - 1, count_y) * size_y
        nxt_b = sides[:, pl.ds(pl.multiple_of(begin + after, 128), size_y)]
        prv_b = sides[:, pl.ds(pl.multiple_of(begin + before, 128), size_y)]
        return jnp.concatenate([own, jnp.where(lane1 < size_y // 2, nxt_b, prv_b)], axis=1)

    def y_side(s):
        body_rows = sides_t[s, pl.ds(pl.multiple_of(row_off + HALO, 8), size_x), :]
        above = sides_t[s, pl.ds(pl.multiple_of(row_off + HALO + size_x, 8), HALO), :]
        below = sides_t[s, pl.ds(row_off, HALO), :]
        return jnp.concatenate([body_rows, above, below], axis=0)

    west, east = x_side(0), x_side(full_y)
    south, north = y_side(0), y_side(1)

    lane2 = lax.broadcasted_iota(jnp.int32, (size_x + 2 * HALO, size_y), 1)
    take_next = lax.rem(lane2, width) >= half
    rain = jnp.zeros((size_x, size_y), f32)
    for l in range(levels):
        g = 0 if l < SPLIT else 1
        if l == groups[g][0]:
            halo_jobs(g, "recv")
            nxt = jnp.concatenate([packed_in[g, 0], diag_in[g, 0, 0], diag_in[g, 1, 0]], axis=0)
            prv = jnp.concatenate([packed_in[g, 1], diag_in[g, 0, 1], diag_in[g, 1, 1]], axis=0)
            mixed = jnp.where(take_next, nxt, prv)

        def extended(f):
            k = f * levels + l
            left = jnp.concatenate([cur[l, f], rows_in[0, l, f], rows_in[1, l, f]], axis=0)
            right = pltpu.roll(mixed, (size_y - (width * k + half)) % size_y, 1)
            return jnp.concatenate([left, right], axis=1)

        def outside(f):
            k = f * levels + l
            value = jnp.where(at_south, south[:, k : k + 1], north[:, k : k + 1])
            value = jnp.where(at_east, east[k : k + 1], value)
            return jnp.where(at_west, west[k : k + 1], value)

        def up(a):
            return pltpu.roll(a, ext_x - 1, 0)

        def down(a):
            return pltpu.roll(a, 1, 0)

        def right_of(a):
            return pltpu.roll(a, ext_y - 1, 1)

        def left_of(a):
            return pltpu.roll(a, 1, 1)

        bh, bu, bv, bq = outside(0), outside(1), outside(2), outside(3)
        h, u, v, q = extended(0), extended(1), extended(2), extended(3)
        h = jnp.where(inside, h, bh)
        q = jnp.where(inside, q, bq)
        for substep in range(ACOUSTIC):
            u = u - acoustic_substep * (up(h) - down(h))
            v = v - acoustic_substep * (right_of(h) - left_of(h))
            u = jnp.where(inside, u, bu)
            v = jnp.where(inside, v, bv)
            h = h - acoustic_substep * ((up(u) - down(u)) + (right_of(v) - left_of(v)))
            h = jnp.where(inside, h, bh)
        flux = (
            jnp.maximum(u, 0.0) * (q - down(q)) + jnp.minimum(u, 0.0) * (up(q) - q)
        ) + (
            jnp.maximum(v, 0.0) * (q - left_of(q)) + jnp.minimum(v, 0.0) * (right_of(q) - q)
        )
        q = (q - drift_step * flux)[0:size_x, 0:size_y]
        fallen = cond_rate[l] * jnp.maximum(q - saturation[l], 0.0)
        q_new = q - fallen
        height_out[0, l] = h[0:size_x, 0:size_y]
        wind_out[0, 0, l] = u[0:size_x, 0:size_y]
        wind_out[0, 1, l] = v[0:size_x, 0:size_y]
        moisture_out[0, l] = q_new
        rain = rain + fallen
        spread = ((wide_here - l * coarse_y) == cells_here).astype(f32)
        summed = lax.dot_general(
            q_new,
            spread,
            (((1,), (1,)), ((), ())),
            precision=lax.Precision.HIGHEST,
            preferred_element_type=f32,
        )
        rows_here = pl.ds(row_off, size_x)
        coarse_rows_buf[rows_here, :] = coarse_rows_buf[rows_here, :] + summed

    coarse_part[...] = jnp.dot(
        row_table,
        coarse_rows_buf[...],
        precision=lax.Precision.HIGHEST,
        preferred_element_type=f32,
    )

    def crs_copy(step, source):
        _, px, py = plane_peer(step)
        return pltpu.make_async_remote_copy(
            src_ref=coarse_part,
            dst_ref=coarse_in.at[source],
            send_sem=crs_send.at[step],
            recv_sem=crs_recv.at[source],
            device_id=(z, px, py),
            device_id_type=MESH,
        )

    for step in range(1, plane):
        crs_copy(step, here).start()
    rain_out[0] = rain

    for half_at, c in enumerate(specs):
        settle(c, coeffs_out.at[0, pl.ds(2 * half_at, 2)])

    total = coarse_part[...]
    for step in range(1, plane):
        other, _, _ = plane_peer(step)
        crs_copy(step, other).wait_recv()
        total = total + coarse_in[other]
    total = total / (row_count * col_count)
    for l in range(levels):
        coarse_out[0, l] = total[:, l * coarse_y : (l + 1) * coarse_y]

    for g in range(2):
        halo_jobs(g, "send")
    for step in range(1, plane):
        rim_copy(step).wait_send()
        crs_copy(step, here).wait_send()
    for step in range(1, count_x):
        rimg_copy(step, ix).wait_send()
    for step in range(1, members):
        rimz_copy(step, z).wait_send()
    for c in rest + specs:
        own_near(c).wait_send()
    own_cross(first).wait_send()

    @pl.when(outer)
    def _():
        own_near(first).wait_send()

    @pl.when(inner)
    def _():
        relay_near(first).wait_send()
        for c in rest + specs:
            sel_inner(c).wait_send()
            sel_outer(c).wait_send()


def write_out(*refs):
    sems = refs[12]
    copies = [pltpu.make_async_copy(refs[n], refs[6 + n], sems.at[n]) for n in range(6)]
    for copy in copies:
        copy.start()
    for copy in copies:
        copy.wait()


def body(
    sizes,
    height,
    wind,
    moisture,
    coeffs,
    damping,
    vmix,
    basis,
    edge_source,
    row_cell,
    col_cell,
    cond_rate,
    saturation,
    ancestry,
):
    members, count_x, count_y = sizes
    plane = count_x * count_y
    _, levels, size_x, size_y = height.shape
    local_k = coeffs.shape[3]
    rim_points = basis.shape[1]
    full_x = row_cell.shape[0]
    full_y = col_cell.shape[0]
    n_edge = edge_source.shape[0]
    coarse_x, coarse_y = full_x // RATIO, full_y // RATIO
    share = 4 * levels // count_x
    rows = 4 * levels
    f32 = jnp.float32
    vmem = pl.BlockSpec(memory_space=pltpu.VMEM)
    dma = pltpu.SemaphoreType.DMA
    coarse_chunk = (coarse_x, levels * coarse_y)
    operands = (
        height,
        wind,
        moisture,
        coeffs,
        damping.reshape(1, -1),
        vmix,
        basis,
        edge_source,
        row_cell.reshape(1, -1),
        col_cell.reshape(1, -1),
        cond_rate,
        saturation,
        ancestry,
    )
    chunks = levels + 2
    scratch = [
        *[pltpu.VMEM(a.shape, a.dtype) for a in operands[3:10]],
        *[pltpu.SMEM(a.shape, a.dtype) for a in operands[10:]],
        pltpu.VMEM((members, levels, 4, size_x, size_y), f32),
        pltpu.VMEM((members, 2, 2, levels, local_k), f32),
        pltpu.VMEM((2, levels, 4, size_x, size_y), f32),
        pltpu.VMEM((2, 2, 2, levels, local_k), f32),
        pltpu.VMEM((4, size_x, size_y), f32),
        pltpu.VMEM((levels, 4, size_x, size_y), f32),
        pltpu.VMEM((2, levels, 4, HALO, size_y), f32),
        pltpu.VMEM((2, levels, 4, HALO, size_y), f32),
        pltpu.VMEM((2, size_x, size_y), f32),
        pltpu.VMEM((2, 2, size_x, size_y), f32),
        pltpu.VMEM((2, 2, 2, HALO, size_y), f32),
        pltpu.VMEM((count_x, share, rim_points), f32),
        pltpu.VMEM((plane, share, rim_points), f32),
        pltpu.VMEM((members, share, rim_points), f32),
        pltpu.VMEM((count_x, share, rim_points), f32),
        pltpu.VMEM((rim_points, n_edge), jnp.bfloat16),
        pltpu.VMEM((rows, n_edge), f32),
        pltpu.VMEM((2, full_x + 2 * HALO, rows), f32),
        pltpu.VMEM((full_x, levels * coarse_y), f32),
        pltpu.VMEM(coarse_chunk, f32),
        pltpu.VMEM((plane, *coarse_chunk), f32),
        dma((2, 8)),
        dma((2, 8)),
        dma((plane,)),
        dma((plane,)),
        dma((members,)),
        dma((members,)),
        dma((count_x,)),
        dma((count_x,)),
        dma((plane,)),
        dma((plane,)),
        dma((chunks, 3)),
        dma((chunks, 3)),
        dma((14,)),
    ]
    outs = (
        pltpu.VMEM(height.shape, f32),
        pltpu.VMEM(wind.shape, f32),
        pltpu.VMEM(moisture.shape, f32),
        pltpu.VMEM((1, size_x, size_y), f32),
        pltpu.VMEM((1, levels, coarse_x, coarse_y), f32),
        pltpu.VMEM(coeffs.shape, f32),
    )
    results = pl.pallas_call(
        functools.partial(kernel, sizes),
        out_shape=outs,
        in_specs=[pl.BlockSpec(memory_space=pltpu.HBM)] * 13,
        out_specs=(vmem,) * 6,
        scratch_shapes=scratch,
        compiler_params=pltpu.CompilerParams(
            collective_id=0, has_side_effects=True, vmem_limit_bytes=36 * 1024 * 1024
        ),
    )(*[pltpu.with_memory_space_constraint(a, pltpu.HBM) for a in operands])
    return pl.pallas_call(
        write_out,
        out_shape=tuple(jax.ShapeDtypeStruct(r.shape, f32) for r in results),
        in_specs=[vmem] * 6,
        out_specs=(pl.BlockSpec(memory_space=pl.ANY),) * 6,
        scratch_shapes=[dma((6,))],
        compiler_params=pltpu.CompilerParams(vmem_limit_bytes=8 * 1024 * 1024),
    )(*results)


def solution(mesh):
    sizes = (mesh.shape["mem"], mesh.shape["gx"], mesh.shape["gy"])
    in_specs = (
        P("mem", None, "gx", "gy"),
        P("mem", None, None, "gx", "gy"),
        P("mem", None, "gx", "gy"),
        P("mem", None, None, ("gx", "gy")),
        P(("gx", "gy")),
        P(),
        P(("gx", "gy"), None),
        P(),
        P(),
        P(),
        P(),
        P(),
        P(),
    )
    out_specs = (
        P("mem", None, "gx", "gy"),
        P("mem", None, None, "gx", "gy"),
        P("mem", None, "gx", "gy"),
        P("mem", "gx", "gy"),
        P("mem", None, None, None),
        P("mem", None, None, ("gx", "gy")),
    )
    return jax.shard_map(
        functools.partial(body, sizes),
        mesh=mesh,
        in_specs=in_specs,
        out_specs=out_specs,
        check_vma=False,
    )
```

profile of v0, /device:TPU:0, one launch (start us, length us, event | category | flops | bytes accessed | tf_op | source)
XLA Modules:
  0.0 29.6 jit_solution(12504391519406413814)
XLA Ops:
  0.6 28.1 %shard_map.172 = (f32[1,4,32,128]{3,2,1,0:T(8,128)S(1)}, f32[1,2,4,32,128]{4,3,2,1,0:T(8,128)S(1)}, f32[1,4,32,128]{3,2,1,0:T(8,128)S(1)}, f32[1,32,128]{2,1,0:T...) custom-call(f32[1,4,32,128]{3,2,1,0:T(8,128)} %height.1, f32[1,2,4,32,128]{4,3,2,1,0:T(8,128)} %wind.1, ...), custom_call_target="tpu_custom_call" | custom-call | tf_op jit(solution)/shard_map/pallas_call | solution.py:715
  28.8 0.8 %shard_map.173 = (f32[1,4,32,128]{3,2,1,0:T(8,128)}, f32[1,2,4,32,128]{4,3,2,1,0:T(8,128)}, f32[1,4,32,128]{3,2,1,0:T(8,128)}, f32[1,32,128]{2,1,0:T(8,128)}, f3...) custom-call(f32[1,4,32,128]{3,2,1,0:T(8,128)S(1)} %get-tuple-element.12.refs_0_, ...), custom_call_target="tpu_custom_call" | custom-call | tf_op jit(solution)/shard_map/pallas_call | solution.py:725
where the time goes:
time: 29.7 us; the launch traced here: 29.6 us
  Pallas kernels  28.9 us (97%)
  between operations  0.65 us (2%)
    pallas_call x1, Pallas kernels, body(): pl.pallas_call(functools.partial(kernel, sizes), out_shape=outs, in_specs...  28.1 us
    pallas_call x1, Pallas kernels, body(): pl.pallas_call(write_out, out_shape=tuple((jax.ShapeDtypeStruct(r.shape,...  0.81 us

commit v1 on v0

--- a/solution.py
+++ b/solution.py
@@ -70,25 +70,17 @@
     coarse_rows_buf,
     coarse_part,
     coarse_in,
-    halo_send,
     halo_recv,
-    rim_send,
-    rim_recv,
-    rimz_send,
-    rimz_recv,
-    rimg_send,
-    rimg_recv,
-    crs_send,
-    crs_recv,
+    batch,
     mem_send,
     mem_recv,
     local,
 ):
     members, count_x, count_y = sizes
     plane = count_x * count_y
-    levels = st.shape[1]
-    size_x = st.shape[3]
-    size_y = st.shape[4]
+    levels = cur.shape[0]
+    size_x = st.shape[2]
+    size_y = st.shape[3]
     full_x = row_cell.shape[1]
     full_y = col_cell.shape[1]
     rim_points = basis.shape[1]
@@ -112,14 +104,15 @@
         other = lax.rem(here + step, plane)
         return other, other // count_y, lax.rem(other, count_y)
 
+    own_slots = pl.ds(z * levels, levels)
     loads = [
         (coeffs_hbm, coeffs),
         (damping_hbm, damping),
         (vmix_hbm, vmix),
-        (height.at[0], st.at[z, :, 0]),
-        (wind.at[0, 0], st.at[z, :, 1]),
-        (wind.at[0, 1], st.at[z, :, 2]),
-        (moisture.at[0], st.at[z, :, 3]),
+        (height.at[0], st.at[own_slots, 0]),
+        (wind.at[0, 0], st.at[own_slots, 1]),
+        (wind.at[0, 1], st.at[own_slots, 2]),
+        (moisture.at[0], st.at[own_slots, 3]),
         (basis_hbm, basis),
         (edge_source_hbm, edge_source),
         (row_cell_hbm, row_cell),
@@ -157,44 +150,44 @@
             acc = acc + vmix[:, j : j + 1] * c[j : j + 1]
         new_fields.append(acc * damping[...])
     for f in range(4):
-        cf[z, f // 2, f % 2] = new_fields[f]
+        cf[2 * z + f // 2, f % 2] = new_fields[f]
     ready(3, 4, 5, 6)
 
     pl.semaphore_wait(barrier, plane - 1 + members - 1)
 
     def chunk(c, slot):
-        return st.at[slot, c] if c < levels else cf.at[slot, c - levels]
+        return st.at[slot * levels + c] if c < levels else cf.at[slot * 2 + c - levels]
 
     def chosen(c, way):
         return st_sel.at[way, c] if c < levels else cf_sel.at[way, c - levels]
 
-    def z_copy(c, kind, src, slot, target, way):
+    def z_copy(c, kind, src, slot, target):
         return pltpu.make_async_remote_copy(
             src_ref=src,
             dst_ref=chunk(c, slot),
-            send_sem=mem_send.at[c, way],
-            recv_sem=mem_recv.at[c, kind],
+            send_sem=mem_send.at[0 if c < levels else 1],
+            recv_sem=mem_recv.at[kind if c == 0 else 1 + 2 * c + kind],
             device_id=(target, ix, iy),
             device_id_type=MESH,
         )
 
     def own_near(c):
-        return z_copy(c, 0, chunk(c, z), z, near, 0)
+        return z_copy(c, 0, chunk(c, z), z, near)
 
     def own_cross(c):
-        return z_copy(c, jnp.where(outer, 2, 1), chunk(c, z), z, cross_inner, 1)
+        return z_copy(c, jnp.where(outer, 2, 1), chunk(c, z), z, cross_inner)
 
     def sel_inner(c):
-        return z_copy(c, 1, chosen(c, 0), z, cross_inner, 1)
+        return z_copy(c, 1, chosen(c, 0), z, cross_inner)
 
     def sel_outer(c):
-        return z_copy(c, 1, chosen(c, 1), z, cross_outer, 2)
+        return z_copy(c, 1, chosen(c, 1), z, cross_outer)
 
     def relay_near(c):
-        return z_copy(c, 0, st_relay, z, near, 0)
+        return z_copy(c, 0, st_relay, z, near)
 
     def arrived(c, kind, slot):
-        z_copy(c, kind, chunk(c, slot), slot, near, 0).wait_recv()
+        z_copy(c, kind, chunk(c, slot), slot, near).wait_recv()
 
     first, rest = 0, list(range(1, levels))
     specs = [levels, levels + 1]
@@ -209,8 +202,7 @@
     def _():
         own_near(rest[0]).start()
         own_cross(first).start()
-        for c in rest[1:] + [first] + specs:
-            own_near(c).start()
+        own_near(rest[1]).start()
 
     low = jnp.concatenate(new_fields, axis=0).astype(jnp.bfloat16)
     ready(7)
@@ -223,8 +215,8 @@
         return pltpu.make_async_remote_copy(
             src_ref=rim_part.at[px],
             dst_ref=rim_in.at[here],
-            send_sem=rim_send.at[step],
-            recv_sem=rim_recv.at[here],
+            send_sem=batch.at[0],
+            recv_sem=batch.at[1],
             device_id=(z, px, py),
             device_id_type=MESH,
         )
@@ -240,13 +232,6 @@
         for way, target in ((0, cross_inner), (1, cross_outer)):
             take_own = ancestry[target] != near
             chosen(c, way)[...] = jnp.where(take_own, chunk(c, z)[...], chunk(c, near)[...])
-
-    @pl.when(inner)
-    def _():
-        c = rest[0]
-        select_near(c)
-        sel_outer(c).start()
-        sel_inner(c).start()
 
     n_edge = edge_source.shape[0]
     table[...] = (
@@ -275,17 +260,21 @@
     wide_here = lax.broadcasted_iota(jnp.int32, (levels * coarse_y, size_y), 0)
     coarse_rows_buf[...] = jnp.zeros_like(coarse_rows_buf)
 
+    def batch_of(n, ref, count):
+        many = ref.at[pl.ds(0, count)]
+        return pltpu.make_async_remote_copy(
+            src_ref=many,
+            dst_ref=many,
+            send_sem=batch.at[n],
+            recv_sem=batch.at[n + 1],
+            device_id=(near, ix, iy),
+            device_id_type=MESH,
+        )
+
+    batch_of(0, rim_in, plane - 1).wait_recv()
     total = rim_part[ix]
     for step in range(1, plane):
-        other, px, py = plane_peer(step)
-        pltpu.make_async_remote_copy(
-            src_ref=rim_part.at[px],
-            dst_ref=rim_in.at[other],
-            send_sem=rim_send.at[step],
-            recv_sem=rim_recv.at[other],
-            device_id=(z, px, py),
-            device_id_type=MESH,
-        ).wait_recv()
+        other, _, _ = plane_peer(step)
         total = total + rim_in[other]
     rim_z[z] = total
 
@@ -293,8 +282,8 @@
         return pltpu.make_async_remote_copy(
             src_ref=rim_z.at[source],
             dst_ref=rim_z.at[source],
-            send_sem=rimz_send.at[step],
-            recv_sem=rimz_recv.at[source],
+            send_sem=batch.at[2],
+            recv_sem=batch.at[3],
             device_id=(lax.rem(z + step, members), ix, iy),
             device_id_type=MESH,
         )
@@ -302,14 +291,22 @@
     for step in range(1, members):
         rimz_copy(step, z).start()
 
+    @pl.when(outer)
+    def _():
+        for c in rest[2:] + [first] + specs:
+            own_near(c).start()
+
     @pl.when(inner)
     def _():
+        select_near(rest[0])
+        sel_outer(rest[0]).start()
+        sel_inner(rest[0]).start()
         arrived(first, 1, cross_inner)
         arrived(first, 2, cross_outer)
         want = ancestry[near]
-        a = st[z, first]
-        a = jnp.where(want == cross_inner, st[cross_inner, first], a)
-        st_relay[...] = jnp.where(want == cross_outer, st[cross_outer, first], a)
+        a = chunk(first, z)[...]
+        a = jnp.where(want == cross_inner, chunk(first, cross_inner)[...], a)
+        st_relay[...] = jnp.where(want == cross_outer, chunk(first, cross_outer)[...], a)
         relay_near(first).start()
         for c in specs:
             own_near(c).start()
@@ -319,10 +316,10 @@
         for c in rest[1:]:
             sel_inner(c).start()
 
+    batch_of(2, rim_z, members - 1).wait_recv()
     share_sel = rim_z[z]
     for step in range(1, members):
         source = lax.rem(z + step, members)
-        rimz_copy(step, source).wait_recv()
         share_sel = jnp.where(mine == source, rim_z[source], share_sel)
     rim_full[ix] = share_sel
 
@@ -330,8 +327,8 @@
         return pltpu.make_async_remote_copy(
             src_ref=rim_full.at[source],
             dst_ref=rim_full.at[source],
-            send_sem=rimg_send.at[step],
-            recv_sem=rimg_recv.at[source],
+            send_sem=batch.at[4],
+            recv_sem=batch.at[5],
             device_id=(z, lax.rem(ix + step, count_x), iy),
             device_id_type=MESH,
         )
@@ -356,14 +353,15 @@
     @pl.when(outer)
     def _():
         arrived(first, 0, near)
-        cur[first] = jnp.where(mine == z, st[z, first], st[near, first])
+        cur[first] = jnp.where(mine == z, chunk(first, z)[...], chunk(first, near)[...])
 
     @pl.when(inner)
     def _():
         arrived(first, 0, near)
-        a = jnp.where(mine == cross_inner, st[cross_inner, first], st[cross_outer, first])
-        a = jnp.where(mine == near, st[near, first], a)
-        cur[first] = jnp.where(mine == z, st[z, first], a)
+        a = chunk(first, cross_outer)[...]
+        a = jnp.where(mine == cross_inner, chunk(first, cross_inner)[...], a)
+        a = jnp.where(mine == near, chunk(first, near)[...], a)
+        cur[first] = jnp.where(mine == z, chunk(first, z)[...], a)
         for c in specs:
             select_near(c)
             sel_outer(c).start()
@@ -404,8 +402,8 @@
                     copy = pltpu.make_async_remote_copy(
                         src_ref=src,
                         dst_ref=dst,
-                        send_sem=halo_send.at[g, base],
-                        recv_sem=halo_recv.at[g, base],
+                        send_sem=local.at[8 * g + base],
+                        recv_sem=halo_recv.at[8 * g + base],
                         device_id=target,
                         device_id_type=MESH,
                     )
@@ -446,8 +444,7 @@
     at_east = gx_pos == full_x
     at_south = gy_pos == -1
 
-    for step in range(1, count_x):
-        rimg_copy(step, lax.rem(ix + step, count_x)).wait_recv()
+    batch_of(4, rim_full, count_x - 1).wait_recv()
     rim = jnp.concatenate([rim_full[g] for g in range(count_x)], axis=0)
     rim_hi = rim.astype(jnp.bfloat16)
     rim_lo = (rim - rim_hi.astype(f32)).astype(jnp.bfloat16)
@@ -563,8 +560,8 @@
         return pltpu.make_async_remote_copy(
             src_ref=coarse_part,
             dst_ref=coarse_in.at[source],
-            send_sem=crs_send.at[step],
-            recv_sem=crs_recv.at[source],
+            send_sem=batch.at[6],
+            recv_sem=batch.at[7],
             device_id=(z, px, py),
             device_id_type=MESH,
         )
@@ -576,10 +573,10 @@
     for half_at, c in enumerate(specs):
         settle(c, coeffs_out.at[0, pl.ds(2 * half_at, 2)])
 
+    batch_of(6, coarse_in, plane - 1).wait_recv()
     total = coarse_part[...]
     for step in range(1, plane):
         other, _, _ = plane_peer(step)
-        crs_copy(step, other).wait_recv()
         total = total + coarse_in[other]
     total = total / (row_count * col_count)
     for l in range(levels):
@@ -587,27 +584,31 @@
 
     for g in range(2):
         halo_jobs(g, "send")
-    for step in range(1, plane):
-        rim_copy(step).wait_send()
-        crs_copy(step, here).wait_send()
-    for step in range(1, count_x):
-        rimg_copy(step, ix).wait_send()
-    for step in range(1, members):
-        rimz_copy(step, z).wait_send()
-    for c in rest + specs:
-        own_near(c).wait_send()
-    own_cross(first).wait_send()
+    batch_of(0, rim_in, plane - 1).wait_send()
+    batch_of(2, rim_z, members - 1).wait_send()
+    batch_of(4, rim_full, count_x - 1).wait_send()
+    batch_of(6, coarse_in, plane - 1).wait_send()
+
+    def sent(n, ref, count):
+        many = ref.at[pl.ds(0, count)]
+        pltpu.make_async_remote_copy(
+            src_ref=many,
+            dst_ref=many,
+            send_sem=mem_send.at[n],
+            recv_sem=mem_recv.at[0],
+            device_id=(near, ix, iy),
+            device_id_type=MESH,
+        ).wait_send()
 
     @pl.when(outer)
     def _():
-        own_near(first).wait_send()
+        sent(0, st, levels + 1)
+        sent(1, cf, 2)
 
     @pl.when(inner)
     def _():
-        relay_near(first).wait_send()
-        for c in rest + specs:
-            sel_inner(c).wait_send()
-            sel_outer(c).wait_send()
+        sent(0, st, 3 * levels - 1)
+        sent(1, cf, 6)
 
 
 def write_out(*refs):
@@ -669,8 +670,8 @@
     scratch = [
         *[pltpu.VMEM(a.shape, a.dtype) for a in operands[3:10]],
         *[pltpu.SMEM(a.shape, a.dtype) for a in operands[10:]],
-        pltpu.VMEM((members, levels, 4, size_x, size_y), f32),
-        pltpu.VMEM((members, 2, 2, levels, local_k), f32),
+        pltpu.VMEM((members * levels, 4, size_x, size_y), f32),
+        pltpu.VMEM((members * 2, 2, levels, local_k), f32),
         pltpu.VMEM((2, levels, 4, size_x, size_y), f32),
         pltpu.VMEM((2, 2, 2, levels, local_k), f32),
         pltpu.VMEM((4, size_x, size_y), f32),
@@ -690,19 +691,11 @@
         pltpu.VMEM((full_x, levels * coarse_y), f32),
         pltpu.VMEM(coarse_chunk, f32),
         pltpu.VMEM((plane, *coarse_chunk), f32),
-        dma((2, 8)),
-        dma((2, 8)),
-        dma((plane,)),
-        dma((plane,)),
-        dma((members,)),
-        dma((members,)),
-        dma((count_x,)),
-        dma((count_x,)),
-        dma((plane,)),
-        dma((plane,)),
-        dma((chunks, 3)),
-        dma((chunks, 3)),
-        dma((14,)),
+        dma((16,)),
+        dma((8,)),
+        dma((2,)),
+        dma((1 + 2 * chunks,)),
+        dma((16,)),
     ]
     outs = (
         pltpu.VMEM(height.shape, f32),

time: 29.7 us -> 28.3 us (0.953)
  Pallas kernels: 28.9 us -> 27.5 us
    pallas_call x1, Pallas kernels: 28.1 us -> 26.7 us  [body(): pl.pallas_call(functools.partial(kernel, sizes), out_shape=outs, in_specs...]
where the time goes in v1:
time: 28.3 us; the launch traced here: 28.1 us
  Pallas kernels  27.5 us (97%)
  between operations  0.65 us (2%)
    pallas_call x1, Pallas kernels, body(): pl.pallas_call(functools.partial(kernel, sizes), out_shape=outs, in_specs...  26.7 us
    pallas_call x1, Pallas kernels, body(): pl.pallas_call(write_out, out_shape=tuple((jax.ShapeDtypeStruct(r.shape,...  0.81 us

profile of v1, /device:TPU:0, one launch (start us, length us, event | category | flops | bytes accessed | tf_op | source)
XLA Modules:
  0.0 28.1 jit_solution(18084592343260289411)
XLA Ops:
  0.6 26.7 %shard_map.172 = (f32[1,4,32,128]{3,2,1,0:T(8,128)S(1)}, f32[1,2,4,32,128]{4,3,2,1,0:T(8,128)S(1)}, f32[1,4,32,128]{3,2,1,0:T(8,128)S(1)}, f32[1,32,128]{2,1,0:T...) custom-call(f32[1,4,32,128]{3,2,1,0:T(8,128)} %height.1, f32[1,2,4,32,128]{4,3,2,1,0:T(8,128)} %wind.1, ...), custom_call_target="tpu_custom_call" | custom-call | tf_op jit(solution)/shard_map/pallas_call | solution.py:708
  27.3 0.8 %shard_map.173 = (f32[1,4,32,128]{3,2,1,0:T(8,128)}, f32[1,2,4,32,128]{4,3,2,1,0:T(8,128)}, f32[1,4,32,128]{3,2,1,0:T(8,128)}, f32[1,32,128]{2,1,0:T(8,128)}, f3...) custom-call(f32[1,4,32,128]{3,2,1,0:T(8,128)S(1)} %get-tuple-element.12.refs_0_, ...), custom_call_target="tpu_custom_call" | custom-call | tf_op jit(solution)/shard_map/pallas_call | solution.py:718

commit v2 on v1

--- a/solution.py
+++ b/solution.py
@@ -10,7 +10,7 @@
 RATIO = 8
 ACOUSTIC = 2
 HALO = 8
-SPLIT = 3
+SPLIT = 2
 
 acoustic_substep = 0.2
 drift_step = 0.4
@@ -75,6 +75,7 @@
     mem_send,
     mem_recv,
     local,
+    rounds,
 ):
     members, count_x, count_y = sizes
     plane = count_x * count_y
@@ -106,13 +107,13 @@
 
     own_slots = pl.ds(z * levels, levels)
     loads = [
-        (coeffs_hbm, coeffs),
-        (damping_hbm, damping),
-        (vmix_hbm, vmix),
         (height.at[0], st.at[own_slots, 0]),
         (wind.at[0, 0], st.at[own_slots, 1]),
         (wind.at[0, 1], st.at[own_slots, 2]),
         (moisture.at[0], st.at[own_slots, 3]),
+        (coeffs_hbm, coeffs),
+        (damping_hbm, damping),
+        (vmix_hbm, vmix),
         (basis_hbm, basis),
         (edge_source_hbm, edge_source),
         (row_cell_hbm, row_cell),
@@ -129,19 +130,103 @@
         for n in which:
             copies[n].wait()
 
+    if plane & (plane - 1):
+        steps = [lax.rem(here + step, plane) for step in range(1, plane)]
+        n_rounds = 2
+    else:
+        n_dims = plane.bit_length() - 1
+        n_rounds = max(n_dims - 1, 2)
+        steps = []
+        for k in range(n_dims):
+            bit = lax.rem(here // 2**k, 2)
+            steps.append(here + 2**k * (1 - 2 * bit))
+
+    def greet(sem, n):
+        for other in steps:
+            pl.semaphore_signal(
+                sem,
+                inc=1,
+                device_id=(z, other // count_y, lax.rem(other, count_y)),
+                device_id_type=MESH,
+            )
+        pl.semaphore_signal(sem, inc=1, device_id=(near, ix, iy), device_id_type=MESH)
+
+        @pl.when(inner)
+        def _():
+            for other in (cross_inner, cross_outer)[:n]:
+                pl.semaphore_signal(
+                    sem, inc=1, device_id=(other, ix, iy), device_id_type=MESH
+                )
+
     barrier = pltpu.get_barrier_semaphore()
-    for step in range(1, plane):
-        _, px, py = plane_peer(step)
-        pl.semaphore_signal(barrier, inc=1, device_id=(z, px, py), device_id_type=MESH)
-    for step in range(1, members):
-        pl.semaphore_signal(
-            barrier,
-            inc=1,
-            device_id=(lax.rem(z + step, members), ix, iy),
+    greet(barrier, 2)
+
+    ready(0, 1, 2, 3)
+
+    pl.semaphore_wait(barrier, len(steps) + 2)
+    greet(rounds.at[0], 1)
+
+    pieces = [(0, pl.ds(0, 4)), (1, pl.ds(0, 2)), (1, pl.ds(2, 2))]
+    pieces += [(l, pl.ds(0, 4)) for l in range(2, levels)]
+    n_pieces = len(pieces)
+
+    def chunk(c, slot):
+        if c >= n_pieces:
+            return cf.at[slot * 2 + c - n_pieces]
+        return st.at[slot * levels + pieces[c][0], pieces[c][1]]
+
+    def chosen(c, way):
+        if c >= n_pieces:
+            return cf_sel.at[way, c - n_pieces]
+        return st_sel.at[way, pieces[c][0], pieces[c][1]]
+
+    def z_copy(c, kind, src, slot, target):
+        return pltpu.make_async_remote_copy(
+            src_ref=src,
+            dst_ref=chunk(c, slot),
+            send_sem=mem_send.at[0 if c < n_pieces else 1],
+            recv_sem=mem_recv.at[kind if c == 0 else 1 + 2 * c + kind],
+            device_id=(target, ix, iy),
             device_id_type=MESH,
         )
 
-    ready(0, 1, 2)
+    def own_near(c):
+        return z_copy(c, 0, chunk(c, z), z, near)
+
+    def own_cross(c):
+        return z_copy(c, jnp.where(outer, 2, 1), chunk(c, z), z, cross_inner)
+
+    def sel_inner(c):
+        return z_copy(c, 1, chosen(c, 0), z, cross_inner)
+
+    def sel_outer(c):
+        return z_copy(c, 1, chosen(c, 1), z, cross_outer)
+
+    def relay_near(c):
+        return z_copy(c, 0, st_relay, z, near)
+
+    def arrived(c, kind, slot):
+        z_copy(c, kind, chunk(c, slot), slot, near).wait_recv()
+
+    first, rest = 0, list(range(1, n_pieces))
+    specs = [n_pieces, n_pieces + 1]
+    lead, later = rest[:2], rest[2:]
+
+    @pl.when(inner)
+    def _():
+        own_cross(first).start()
+        for c in rest:
+            own_near(c).start()
+
+    @pl.when(outer)
+    def _():
+        for c in lead:
+            own_near(c).start()
+        own_cross(first).start()
+        for c in later:
+            own_near(c).start()
+
+    ready(4, 5, 6)
     new_fields = []
     for f in range(4):
         c = coeffs[0, f]
@@ -151,59 +236,11 @@
         new_fields.append(acc * damping[...])
     for f in range(4):
         cf[2 * z + f // 2, f % 2] = new_fields[f]
-    ready(3, 4, 5, 6)
-
-    pl.semaphore_wait(barrier, plane - 1 + members - 1)
-
-    def chunk(c, slot):
-        return st.at[slot * levels + c] if c < levels else cf.at[slot * 2 + c - levels]
-
-    def chosen(c, way):
-        return st_sel.at[way, c] if c < levels else cf_sel.at[way, c - levels]
-
-    def z_copy(c, kind, src, slot, target):
-        return pltpu.make_async_remote_copy(
-            src_ref=src,
-            dst_ref=chunk(c, slot),
-            send_sem=mem_send.at[0 if c < levels else 1],
-            recv_sem=mem_recv.at[kind if c == 0 else 1 + 2 * c + kind],
-            device_id=(target, ix, iy),
-            device_id_type=MESH,
-        )
-
-    def own_near(c):
-        return z_copy(c, 0, chunk(c, z), z, near)
-
-    def own_cross(c):
-        return z_copy(c, jnp.where(outer, 2, 1), chunk(c, z), z, cross_inner)
-
-    def sel_inner(c):
-        return z_copy(c, 1, chosen(c, 0), z, cross_inner)
-
-    def sel_outer(c):
-        return z_copy(c, 1, chosen(c, 1), z, cross_outer)
-
-    def relay_near(c):
-        return z_copy(c, 0, st_relay, z, near)
-
-    def arrived(c, kind, slot):
-        z_copy(c, kind, chunk(c, slot), slot, near).wait_recv()
-
-    first, rest = 0, list(range(1, levels))
-    specs = [levels, levels + 1]
-
-    @pl.when(inner)
-    def _():
-        own_cross(first).start()
-        for c in rest:
-            own_near(c).start()
-
-    @pl.when(outer)
-    def _():
-        own_near(rest[0]).start()
-        own_cross(first).start()
-        own_near(rest[1]).start()
-
+    pl.semaphore_wait(rounds.at[0], len(steps) + jnp.where(inner, 2, 1))
+    for k in range(1, n_rounds):
+        greet(rounds.at[k], 0)
+        if k < n_rounds - 1:
+            pl.semaphore_wait(rounds.at[k], len(steps) + 1)
     low = jnp.concatenate(new_fields, axis=0).astype(jnp.bfloat16)
     ready(7)
     part = jnp.dot(low, basis[...], preferred_element_type=f32)
@@ -221,6 +258,7 @@
             device_id_type=MESH,
         )
 
+    pl.semaphore_wait(rounds.at[n_rounds - 1], len(steps) + 1)
     for step in range(1, plane):
         rim_copy(step).start()
 
@@ -260,6 +298,13 @@
     wide_here = lax.broadcasted_iota(jnp.int32, (levels * coarse_y, size_y), 0)
     coarse_rows_buf[...] = jnp.zeros_like(coarse_rows_buf)
 
+    @pl.when(inner)
+    def _():
+        for c in lead:
+            select_near(c)
+            sel_outer(c).start()
+            sel_inner(c).start()
+
     def batch_of(n, ref, count):
         many = ref.at[pl.ds(0, count)]
         return pltpu.make_async_remote_copy(
@@ -293,14 +338,11 @@
 
     @pl.when(outer)
     def _():
-        for c in rest[2:] + [first] + specs:
+        for c in [first] + specs:
             own_near(c).start()
 
     @pl.when(inner)
     def _():
-        select_near(rest[0])
-        sel_outer(rest[0]).start()
-        sel_inner(rest[0]).start()
         arrived(first, 1, cross_inner)
         arrived(first, 2, cross_outer)
         want = ancestry[near]
@@ -308,12 +350,10 @@
         a = jnp.where(want == cross_inner, chunk(first, cross_inner)[...], a)
         st_relay[...] = jnp.where(want == cross_outer, chunk(first, cross_outer)[...], a)
         relay_near(first).start()
-        for c in specs:
-            own_near(c).start()
-        for c in rest[1:]:
+        for c in later:
             select_near(c)
             sel_outer(c).start()
-        for c in rest[1:]:
+        for c in later:
             sel_inner(c).start()
 
     batch_of(2, rim_z, members - 1).wait_recv()
@@ -336,6 +376,12 @@
     for step in range(1, count_x):
         rimg_copy(step, ix).start()
 
+    @pl.when(inner)
+    def _():
+        arrived(first, 0, near)
+        for c in specs:
+            own_near(c).start()
+
     lane = lax.broadcasted_iota(jnp.int32, (size_x, size_y), 1)
     width = size_y // (4 * levels)
     half = width // 2
@@ -350,29 +396,11 @@
         a = jnp.where(mine == z, chunk(c, z)[...], chunk(c, cross_inner)[...])
         ref[...] = jnp.where(mine == near, chunk(c, near)[...], a)
 
-    @pl.when(outer)
-    def _():
-        arrived(first, 0, near)
-        cur[first] = jnp.where(mine == z, chunk(first, z)[...], chunk(first, near)[...])
-
-    @pl.when(inner)
-    def _():
-        arrived(first, 0, near)
-        a = chunk(first, cross_outer)[...]
-        a = jnp.where(mine == cross_inner, chunk(first, cross_inner)[...], a)
-        a = jnp.where(mine == near, chunk(first, near)[...], a)
-        cur[first] = jnp.where(mine == z, chunk(first, z)[...], a)
-        for c in specs:
-            select_near(c)
-            sel_outer(c).start()
-        for c in specs:
-            sel_inner(c).start()
-
-    groups = [list(range(SPLIT)), list(range(SPLIT, levels))]
+    order = list(range(1, levels - 1)) + [first, levels - 1]
+    groups = [order[:SPLIT], order[SPLIT:]]
 
     def halo_jobs(g, mode):
-        lo, n_lev = groups[g][0], len(groups[g])
-        lev = pl.ds(lo, n_lev)
+        lev = pl.ds(SPLIT * g, len(groups[g]))
         for dx in (-1, 0, 1):
             for dy in (-1, 0, 1):
                 if dx == 0 and dy == 0:
@@ -420,10 +448,12 @@
         pack = jnp.zeros((size_x, size_y), f32)
         for l in groups[g]:
             if l != first:
-                settle(l, cur.at[l])
+                for c in range(n_pieces):
+                    if pieces[c][0] == l:
+                        settle(c, cur.at[l, pieces[c][1]])
             for f in range(4):
-                rows_out[0, l, f] = cur[l, f, 0:HALO]
-                rows_out[1, l, f] = cur[l, f, size_x - HALO :]
+                rows_out[0, order.index(l), f] = cur[l, f, 0:HALO]
+                rows_out[1, order.index(l), f] = cur[l, f, size_x - HALO :]
                 k = f * levels + l
                 moved = pltpu.roll(cur[l, f], (width * k + half) % size_y, 1)
                 pack = jnp.where(lane // width == k, moved, pack)
@@ -431,6 +461,27 @@
         halo_jobs(g, "start")
 
     halo_out(0)
+
+    @pl.when(inner)
+    def _():
+        for c in specs:
+            select_near(c)
+            sel_outer(c).start()
+        for c in specs:
+            sel_inner(c).start()
+
+    @pl.when(outer)
+    def _():
+        arrived(first, 0, near)
+        cur[first] = jnp.where(mine == z, chunk(first, z)[...], chunk(first, near)[...])
+
+    @pl.when(inner)
+    def _():
+        a = chunk(first, cross_outer)[...]
+        a = jnp.where(mine == cross_inner, chunk(first, cross_inner)[...], a)
+        a = jnp.where(mine == near, chunk(first, near)[...], a)
+        cur[first] = jnp.where(mine == z, chunk(first, z)[...], a)
+
     halo_out(1)
 
     ext_x = size_x + 2 * HALO
@@ -480,9 +531,10 @@
 
     lane2 = lax.broadcasted_iota(jnp.int32, (size_x + 2 * HALO, size_y), 1)
     take_next = lax.rem(lane2, width) >= half
-    rain = jnp.zeros((size_x, size_y), f32)
-    for l in range(levels):
-        g = 0 if l < SPLIT else 1
+    rains = {}
+    for l in order:
+        at = order.index(l)
+        g = at // SPLIT
         if l == groups[g][0]:
             halo_jobs(g, "recv")
             nxt = jnp.concatenate([packed_in[g, 0], diag_in[g, 0, 0], diag_in[g, 1, 0]], axis=0)
@@ -491,7 +543,7 @@
 
         def extended(f):
             k = f * levels + l
-            left = jnp.concatenate([cur[l, f], rows_in[0, l, f], rows_in[1, l, f]], axis=0)
+            left = jnp.concatenate([cur[l, f], rows_in[0, at, f], rows_in[1, at, f]], axis=0)
             right = pltpu.roll(mixed, (size_y - (width * k + half)) % size_y, 1)
             return jnp.concatenate([left, right], axis=1)
 
@@ -536,7 +588,7 @@
         wind_out[0, 0, l] = u[0:size_x, 0:size_y]
         wind_out[0, 1, l] = v[0:size_x, 0:size_y]
         moisture_out[0, l] = q_new
-        rain = rain + fallen
+        rains[l] = fallen
         spread = ((wide_here - l * coarse_y) == cells_here).astype(f32)
         summed = lax.dot_general(
             q_new,
@@ -568,6 +620,9 @@
 
     for step in range(1, plane):
         crs_copy(step, here).start()
+    rain = rains[0]
+    for l in range(1, levels):
+        rain = rain + rains[l]
     rain_out[0] = rain
 
     for half_at, c in enumerate(specs):
@@ -666,7 +721,7 @@
         saturation,
         ancestry,
     )
-    chunks = levels + 2
+    chunks = levels + 3
     scratch = [
         *[pltpu.VMEM(a.shape, a.dtype) for a in operands[3:10]],
         *[pltpu.SMEM(a.shape, a.dtype) for a in operands[10:]],
@@ -696,6 +751,7 @@
         dma((2,)),
         dma((1 + 2 * chunks,)),
         dma((16,)),
+        pltpu.SemaphoreType.REGULAR((max(plane.bit_length() - 2, 2),)),
     ]
     outs = (
         pltpu.VMEM(height.shape, f32),

time: 28.3 us -> 27.2 us (0.961)
  Pallas kernels: 27.5 us -> 26.4 us
    pallas_call x1, Pallas kernels: 26.7 us -> 25.6 us  [body(): pl.pallas_call(functools.partial(kernel, sizes), out_shape=outs, in_specs...]
where the time goes in v2:
time: 27.2 us; the launch traced here: 27.1 us
  Pallas kernels  26.4 us (97%)
  between operations  0.65 us (2%)
    pallas_call x1, Pallas kernels, body(): pl.pallas_call(functools.partial(kernel, sizes), out_shape=outs, in_specs...  25.6 us
    pallas_call x1, Pallas kernels, body(): pl.pallas_call(write_out, out_shape=tuple((jax.ShapeDtypeStruct(r.shape,...  0.81 us

profile of v2, /device:TPU:0, one launch (start us, length us, event | category | flops | bytes accessed | tf_op | source)
XLA Modules:
  0.0 27.1 jit_solution(10743932762252401744)
XLA Ops:
  0.6 25.6 %shard_map.172 = (f32[1,4,32,128]{3,2,1,0:T(8,128)S(1)}, f32[1,2,4,32,128]{4,3,2,1,0:T(8,128)S(1)}, f32[1,4,32,128]{3,2,1,0:T(8,128)S(1)}, f32[1,32,128]{2,1,0:T...) custom-call(f32[1,4,32,128]{3,2,1,0:T(8,128)} %height.1, f32[1,2,4,32,128]{4,3,2,1,0:T(8,128)} %wind.1, ...), custom_call_target="tpu_custom_call" | custom-call | tf_op jit(solution)/shard_map/pallas_call | solution.py:764
  26.3 0.8 %shard_map.173 = (f32[1,4,32,128]{3,2,1,0:T(8,128)}, f32[1,2,4,32,128]{4,3,2,1,0:T(8,128)}, f32[1,4,32,128]{3,2,1,0:T(8,128)}, f32[1,32,128]{2,1,0:T(8,128)}, f3...) custom-call(f32[1,4,32,128]{3,2,1,0:T(8,128)S(1)} %get-tuple-element.12.refs_0_, ...), custom_call_target="tpu_custom_call" | custom-call | tf_op jit(solution)/shard_map/pallas_call | solution.py:774

commit v3 on v2

--- a/solution.py
+++ b/solution.py
@@ -67,6 +67,8 @@
     table,
     sides,
     sides_t,
+    spread,
+    row_table3,
     coarse_rows_buf,
     coarse_part,
     coarse_in,
@@ -297,6 +299,8 @@
     cells_here = col_cell[:, pl.ds(col_off, size_y)]
     wide_here = lax.broadcasted_iota(jnp.int32, (levels * coarse_y, size_y), 0)
     coarse_rows_buf[...] = jnp.zeros_like(coarse_rows_buf)
+    for m in range(3):
+        row_table3[:, m * full_x : (m + 1) * full_x] = row_table.astype(jnp.bfloat16)
 
     @pl.when(inner)
     def _():
@@ -398,13 +402,16 @@
 
     order = list(range(1, levels - 1)) + [first, levels - 1]
     groups = [order[:SPLIT], order[SPLIT:]]
+    for n, l in enumerate(order):
+        hit = ((wide_here - l * coarse_y) == cells_here).astype(f32).astype(jnp.bfloat16)
+        for m in range(3):
+            spread[:, (3 * n + m) * size_y : (3 * n + m + 1) * size_y] = hit
 
     def halo_jobs(g, mode):
         lev = pl.ds(SPLIT * g, len(groups[g]))
-        for dx in (-1, 0, 1):
-            for dy in (-1, 0, 1):
-                if dx == 0 and dy == 0:
-                    continue
+        toward = [(-1, -1), (0, -1), (-1, 0), (1, -1), (-1, 1), (0, 1), (1, 1), (1, 0)]
+        for dx, dy in toward:
+            if True:
                 flip = -1 if mode == "recv" else 1
                 ok = jnp.bool_(True)
                 if dx * flip == -1:
@@ -490,10 +497,17 @@
     cpos = lax.broadcasted_iota(jnp.int32, (ext_x, ext_y), 1)
     gx_pos = ix * size_x + jnp.where(rpos < size_x + HALO, rpos, rpos - ext_x)
     gy_pos = iy * size_y + jnp.where(cpos < size_y + size_y // 2, cpos, cpos - ext_y)
-    inside = (gx_pos >= 0) & (gx_pos < full_x) & (gy_pos >= 0) & (gy_pos < full_y)
-    at_west = gx_pos == -1
-    at_east = gx_pos == full_x
-    at_south = gy_pos == -1
+    beside = slice(size_y, ext_y)
+    above = slice(size_x, size_x + HALO)
+    below = slice(size_x + HALO, ext_x)
+    has_up = ix < count_x - 1
+    has_down = ix > 0
+
+    def inside(rows):
+        xs, ys = gx_pos[rows, beside], gy_pos[rows, beside]
+        return (xs >= 0) & (xs < full_x) & (ys >= 0) & (ys < full_y)
+
+    in_main, in_up, in_down = inside(slice(0, size_x)), inside(above), inside(below)
 
     batch_of(4, rim_full, count_x - 1).wait_recv()
     rim = jnp.concatenate([rim_full[g] for g in range(count_x)], axis=0)
@@ -528,10 +542,22 @@
 
     west, east = x_side(0), x_side(full_y)
     south, north = y_side(0), y_side(1)
+    if count_y > 1:
+        column = jnp.where(iy == 0, south, north)
 
     lane2 = lax.broadcasted_iota(jnp.int32, (size_x + 2 * HALO, size_y), 1)
     take_next = lax.rem(lane2, width) >= half
     rains = {}
+    thirds = []
+    summed = jnp.zeros((size_x, levels * coarse_y), f32)
+
+    def split(a):
+        parts = []
+        for _ in range(3):
+            parts.append(a.astype(jnp.bfloat16))
+            a = a - parts[-1].astype(f32)
+        return parts
+
     for l in order:
         at = order.index(l)
         g = at // SPLIT
@@ -547,11 +573,38 @@
             right = pltpu.roll(mixed, (size_y - (width * k + half)) % size_y, 1)
             return jnp.concatenate([left, right], axis=1)
 
-        def outside(f):
+        def frame(f):
             k = f * levels + l
-            value = jnp.where(at_south, south[:, k : k + 1], north[:, k : k + 1])
-            value = jnp.where(at_east, east[k : k + 1], value)
-            return jnp.where(at_west, west[k : k + 1], value)
+            if count_y > 1:
+                side = jnp.broadcast_to(column[:, k : k + 1], (ext_x, size_y))
+            else:
+                at_south = gy_pos[:, beside] < 0
+                side = jnp.where(at_south, south[:, k : k + 1], north[:, k : k + 1])
+            eastern = jnp.broadcast_to(east[k : k + 1], (HALO, ext_y))
+            western = jnp.broadcast_to(west[k : k + 1], (HALO, ext_y))
+            up_v = jnp.where(has_up, side[above], eastern[:, beside])
+            down_v = jnp.where(has_down, side[below], western[:, beside])
+
+            def put(a):
+                left = jnp.concatenate(
+                    [
+                        a[0:size_x, 0:size_y],
+                        jnp.where(has_up, a[above, 0:size_y], eastern[:, 0:size_y]),
+                        jnp.where(has_down, a[below, 0:size_y], western[:, 0:size_y]),
+                    ],
+                    axis=0,
+                )
+                right = jnp.concatenate(
+                    [
+                        jnp.where(in_main, a[0:size_x, beside], side[0:size_x]),
+                        jnp.where(in_up, a[above, beside], up_v),
+                        jnp.where(in_down, a[below, beside], down_v),
+                    ],
+                    axis=0,
+                )
+                return jnp.concatenate([left, right], axis=1)
+
+            return put
 
         def up(a):
             return pltpu.roll(a, ext_x - 1, 0)
@@ -565,17 +618,17 @@
         def left_of(a):
             return pltpu.roll(a, 1, 1)
 
-        bh, bu, bv, bq = outside(0), outside(1), outside(2), outside(3)
+        put_h, put_u, put_v, put_q = frame(0), frame(1), frame(2), frame(3)
         h, u, v, q = extended(0), extended(1), extended(2), extended(3)
-        h = jnp.where(inside, h, bh)
-        q = jnp.where(inside, q, bq)
+        h = put_h(h)
+        q = put_q(q)
         for substep in range(ACOUSTIC):
             u = u - acoustic_substep * (up(h) - down(h))
             v = v - acoustic_substep * (right_of(h) - left_of(h))
-            u = jnp.where(inside, u, bu)
-            v = jnp.where(inside, v, bv)
+            u = put_u(u)
+            v = put_v(v)
             h = h - acoustic_substep * ((up(u) - down(u)) + (right_of(v) - left_of(v)))
-            h = jnp.where(inside, h, bh)
+            h = put_h(h)
         flux = (
             jnp.maximum(u, 0.0) * (q - down(q)) + jnp.minimum(u, 0.0) * (up(q) - q)
         ) + (
@@ -589,37 +642,37 @@
         wind_out[0, 1, l] = v[0:size_x, 0:size_y]
         moisture_out[0, l] = q_new
         rains[l] = fallen
-        spread = ((wide_here - l * coarse_y) == cells_here).astype(f32)
-        summed = lax.dot_general(
-            q_new,
-            spread,
-            (((1,), (1,)), ((), ())),
-            precision=lax.Precision.HIGHEST,
-            preferred_element_type=f32,
-        )
-        rows_here = pl.ds(row_off, size_x)
-        coarse_rows_buf[rows_here, :] = coarse_rows_buf[rows_here, :] + summed
-
+        thirds += split(q_new)
+        if l == groups[g][-1]:
+            span = spread[:, 3 * size_y * (at + 1 - len(groups[g])) : 3 * size_y * (at + 1)]
+            summed = summed + lax.dot_general(
+                jnp.concatenate(thirds, axis=1),
+                span,
+                (((1,), (1,)), ((), ())),
+                preferred_element_type=f32,
+            )
+            thirds = []
+
+    for n, third in enumerate(split(summed)):
+        start = pl.multiple_of(n * full_x + row_off, 16)
+        coarse_rows_buf[pl.ds(start, size_x), :] = third
     coarse_part[...] = jnp.dot(
-        row_table,
-        coarse_rows_buf[...],
-        precision=lax.Precision.HIGHEST,
-        preferred_element_type=f32,
+        row_table3[...], coarse_rows_buf[...], preferred_element_type=f32
     )
 
-    def crs_copy(step, source):
-        _, px, py = plane_peer(step)
+    def crs_copy(other):
+        px, py = other // count_y, other % count_y
         return pltpu.make_async_remote_copy(
             src_ref=coarse_part,
-            dst_ref=coarse_in.at[source],
+            dst_ref=coarse_in.at[here],
             send_sem=batch.at[6],
             recv_sem=batch.at[7],
             device_id=(z, px, py),
             device_id_type=MESH,
         )
 
-    for step in range(1, plane):
-        crs_copy(step, here).start()
+    for other in range(plane):
+        pl.when(here != other)(crs_copy(other).start)
     rain = rains[0]
     for l in range(1, levels):
         rain = rain + rains[l]
@@ -743,7 +796,9 @@
         pltpu.VMEM((rim_points, n_edge), jnp.bfloat16),
         pltpu.VMEM((rows, n_edge), f32),
         pltpu.VMEM((2, full_x + 2 * HALO, rows), f32),
-        pltpu.VMEM((full_x, levels * coarse_y), f32),
+        pltpu.VMEM((levels * coarse_y, 3 * levels * size_y), jnp.bfloat16),
+        pltpu.VMEM((coarse_x, 3 * full_x), jnp.bfloat16),
+        pltpu.VMEM((3 * full_x, levels * coarse_y), jnp.bfloat16),
         pltpu.VMEM(coarse_chunk, f32),
         pltpu.VMEM((plane, *coarse_chunk), f32),
         dma((16,)),

time: 27.2 us -> 26.8 us (0.985)
  Pallas kernels: 26.4 us -> 26 us
    pallas_call x1, Pallas kernels: 25.6 us -> 25.2 us  [body(): pl.pallas_call(functools.partial(kernel, sizes), out_shape=outs, in_specs...]
where the time goes in v3:
time: 26.8 us; the launch traced here: 26.6 us
  Pallas kernels  26 us (97%)
  between operations  0.65 us (2%)
    pallas_call x1, Pallas kernels, body(): pl.pallas_call(functools.partial(kernel, sizes), out_shape=outs, in_specs...  25.2 us
    pallas_call x1, Pallas kernels, body(): pl.pallas_call(write_out, out_shape=tuple((jax.ShapeDtypeStruct(r.shape,...  0.81 us

profile of v3, /device:TPU:0, one launch (start us, length us, event | category | flops | bytes accessed | tf_op | source)
XLA Modules:
  0.0 26.6 jit_solution(18235494995626483481)
XLA Ops:
  0.6 25.2 %shard_map.172 = (f32[1,4,32,128]{3,2,1,0:T(8,128)S(1)}, f32[1,2,4,32,128]{4,3,2,1,0:T(8,128)S(1)}, f32[1,4,32,128]{3,2,1,0:T(8,128)S(1)}, f32[1,32,128]{2,1,0:T...) custom-call(f32[1,4,32,128]{3,2,1,0:T(8,128)} %height.1, f32[1,2,4,32,128]{4,3,2,1,0:T(8,128)} %wind.1, ...), custom_call_target="tpu_custom_call" | custom-call | tf_op jit(solution)/shard_map/pallas_call | solution.py:819
  25.8 0.8 %shard_map.173 = (f32[1,4,32,128]{3,2,1,0:T(8,128)}, f32[1,2,4,32,128]{4,3,2,1,0:T(8,128)}, f32[1,4,32,128]{3,2,1,0:T(8,128)}, f32[1,32,128]{2,1,0:T(8,128)}, f3...) custom-call(f32[1,4,32,128]{3,2,1,0:T(8,128)S(1)} %get-tuple-element.12.refs_0_, ...), custom_call_target="tpu_custom_call" | custom-call | tf_op jit(solution)/shard_map/pallas_call | solution.py:829

commit v4 on v3

--- a/solution.py
+++ b/solution.py
@@ -424,7 +424,7 @@
                     ok = jnp.logical_and(ok, iy < count_y - 1)
                 sx = 0 if dx == -1 else 1
                 sy = 0 if dy == -1 else 1
-                rows = pl.ds(0, HALO) if dx == -1 else pl.ds(size_x - HALO, HALO)
+                rows = pl.ds(0, HALO) if dx == -1 else pl.ds(size_x // 2 - HALO, HALO)
                 if dy == 0:
                     src, dst, base = rows_out.at[sx, lev], rows_in.at[sx, lev], sx
                 elif dx == 0:
@@ -451,6 +451,8 @@
 
                 pl.when(ok)(go)
 
+    fold = size_x // 2
+
     def halo_out(g):
         pack = jnp.zeros((size_x, size_y), f32)
         for l in groups[g]:
@@ -461,10 +463,11 @@
             for f in range(4):
                 rows_out[0, order.index(l), f] = cur[l, f, 0:HALO]
                 rows_out[1, order.index(l), f] = cur[l, f, size_x - HALO :]
-                k = f * levels + l
+                k = f * len(groups[g]) + groups[g].index(l)
                 moved = pltpu.roll(cur[l, f], (width * k + half) % size_y, 1)
                 pack = jnp.where(lane // width == k, moved, pack)
-        packed[g] = pack
+        below_half = pltpu.roll(pack[fold:], size_y // 2, 1)
+        packed[g] = jnp.where(lane[:fold] < size_y // 2, pack[:fold], below_half)
         halo_jobs(g, "start")
 
     halo_out(0)
@@ -563,12 +566,18 @@
         g = at // SPLIT
         if l == groups[g][0]:
             halo_jobs(g, "recv")
-            nxt = jnp.concatenate([packed_in[g, 0], diag_in[g, 0, 0], diag_in[g, 1, 0]], axis=0)
-            prv = jnp.concatenate([packed_in[g, 1], diag_in[g, 0, 1], diag_in[g, 1, 1]], axis=0)
-            mixed = jnp.where(take_next, nxt, prv)
+
+
+            def unfold(way):
+                part = packed_in[g, way]
+                turned = pltpu.roll(part, size_y // 2, 1)
+                corner = pltpu.roll(diag_in[g, 1, way], size_y // 2, 1)
+                return jnp.concatenate([part, turned, diag_in[g, 0, way], corner], axis=0)
+
+            mixed = jnp.where(take_next, unfold(0), unfold(1))
 
         def extended(f):
-            k = f * levels + l
+            k = f * len(groups[g]) + groups[g].index(l)
             left = jnp.concatenate([cur[l, f], rows_in[0, at, f], rows_in[1, at, f]], axis=0)
             right = pltpu.roll(mixed, (size_y - (width * k + half)) % size_y, 1)
             return jnp.concatenate([left, right], axis=1)
@@ -681,21 +690,11 @@
     for half_at, c in enumerate(specs):
         settle(c, coeffs_out.at[0, pl.ds(2 * half_at, 2)])
 
-    batch_of(6, coarse_in, plane - 1).wait_recv()
-    total = coarse_part[...]
-    for step in range(1, plane):
-        other, _, _ = plane_peer(step)
-        total = total + coarse_in[other]
-    total = total / (row_count * col_count)
-    for l in range(levels):
-        coarse_out[0, l] = total[:, l * coarse_y : (l + 1) * coarse_y]
-
     for g in range(2):
         halo_jobs(g, "send")
     batch_of(0, rim_in, plane - 1).wait_send()
     batch_of(2, rim_z, members - 1).wait_send()
     batch_of(4, rim_full, count_x - 1).wait_send()
-    batch_of(6, coarse_in, plane - 1).wait_send()
 
     def sent(n, ref, count):
         many = ref.at[pl.ds(0, count)]
@@ -717,6 +716,17 @@
     def _():
         sent(0, st, 3 * levels - 1)
         sent(1, cf, 6)
+
+    batch_of(6, coarse_in, plane - 1).wait_recv()
+    total = coarse_part[...]
+    for step in range(1, plane):
+        other, _, _ = plane_peer(step)
+        total = total + coarse_in[other]
+    total = total / (row_count * col_count)
+    for l in range(levels):
+        coarse_out[0, l] = total[:, l * coarse_y : (l + 1) * coarse_y]
+
+    batch_of(6, coarse_in, plane - 1).wait_send()
 
 
 def write_out(*refs):
@@ -786,8 +796,8 @@
         pltpu.VMEM((levels, 4, size_x, size_y), f32),
         pltpu.VMEM((2, levels, 4, HALO, size_y), f32),
         pltpu.VMEM((2, levels, 4, HALO, size_y), f32),
-        pltpu.VMEM((2, size_x, size_y), f32),
-        pltpu.VMEM((2, 2, size_x, size_y), f32),
+        pltpu.VMEM((2, size_x // 2, size_y), f32),
+        pltpu.VMEM((2, 2, size_x // 2, size_y), f32),
         pltpu.VMEM((2, 2, 2, HALO, size_y), f32),
         pltpu.VMEM((count_x, share, rim_points), f32),
         pltpu.VMEM((plane, share, rim_points), f32),

time: 26.8 us -> 26.7 us (level)
  no operation moved by 1% of the time
where the time goes in v4:
time: 26.7 us; the launch traced here: 26.6 us
  Pallas kernels  25.9 us (97%)
  between operations  0.65 us (2%)
    pallas_call x1, Pallas kernels, body(): pl.pallas_call(functools.partial(kernel, sizes), out_shape=outs, in_specs...  25.1 us
    pallas_call x1, Pallas kernels, body(): pl.pallas_call(write_out, out_shape=tuple((jax.ShapeDtypeStruct(r.shape,...  0.81 us

profile of v4, /device:TPU:0, one launch (start us, length us, event | category | flops | bytes accessed | tf_op | source)
XLA Modules:
  0.0 26.6 jit_solution(3430514069117251024)
XLA Ops:
  0.6 25.1 %shard_map.172 = (f32[1,4,32,128]{3,2,1,0:T(8,128)S(1)}, f32[1,2,4,32,128]{4,3,2,1,0:T(8,128)S(1)}, f32[1,4,32,128]{3,2,1,0:T(8,128)S(1)}, f32[1,32,128]{2,1,0:T...) custom-call(f32[1,4,32,128]{3,2,1,0:T(8,128)} %height.1, f32[1,2,4,32,128]{4,3,2,1,0:T(8,128)} %wind.1, ...), custom_call_target="tpu_custom_call" | custom-call | tf_op jit(solution)/shard_map/pallas_call | solution.py:829
  25.7 0.8 %shard_map.173 = (f32[1,4,32,128]{3,2,1,0:T(8,128)}, f32[1,2,4,32,128]{4,3,2,1,0:T(8,128)}, f32[1,4,32,128]{3,2,1,0:T(8,128)}, f32[1,32,128]{2,1,0:T(8,128)}, f3...) custom-call(f32[1,4,32,128]{3,2,1,0:T(8,128)S(1)} %get-tuple-element.12.refs_0_, ...), custom_call_target="tpu_custom_call" | custom-call | tf_op jit(solution)/shard_map/pallas_call | solution.py:839

commit v5 on v4

--- a/solution.py
+++ b/solution.py
@@ -307,6 +307,7 @@
         for c in lead:
             select_near(c)
             sel_outer(c).start()
+        for c in lead:
             sel_inner(c).start()
 
     def batch_of(n, ref, count):

time: 26.7 us -> 26.8 us (level)
  no operation moved by 1% of the time
where the time goes in v5:
time: 26.8 us; the launch traced here: 26.7 us
  Pallas kernels  26 us (97%)
  between operations  0.65 us (2%)
    pallas_call x1, Pallas kernels, body(): pl.pallas_call(functools.partial(kernel, sizes), out_shape=outs, in_specs...  25.2 us
    pallas_call x1, Pallas kernels, body(): pl.pallas_call(write_out, out_shape=tuple((jax.ShapeDtypeStruct(r.shape,...  0.81 us

profile of v5, /device:TPU:0, one launch (start us, length us, event | category | flops | bytes accessed | tf_op | source)
XLA Modules:
  0.0 26.7 jit_solution(17818303772236517550)
XLA Ops:
  0.6 25.2 %shard_map.172 = (f32[1,4,32,128]{3,2,1,0:T(8,128)S(1)}, f32[1,2,4,32,128]{4,3,2,1,0:T(8,128)S(1)}, f32[1,4,32,128]{3,2,1,0:T(8,128)S(1)}, f32[1,32,128]{2,1,0:T...) custom-call(f32[1,4,32,128]{3,2,1,0:T(8,128)} %height.1, f32[1,2,4,32,128]{4,3,2,1,0:T(8,128)} %wind.1, ...), custom_call_target="tpu_custom_call" | custom-call | tf_op jit(solution)/shard_map/pallas_call | solution.py:830
  25.8 0.8 %shard_map.173 = (f32[1,4,32,128]{3,2,1,0:T(8,128)}, f32[1,2,4,32,128]{4,3,2,1,0:T(8,128)}, f32[1,4,32,128]{3,2,1,0:T(8,128)}, f32[1,32,128]{2,1,0:T(8,128)}, f3...) custom-call(f32[1,4,32,128]{3,2,1,0:T(8,128)S(1)} %get-tuple-element.12.refs_0_, ...), custom_call_target="tpu_custom_call" | custom-call | tf_op jit(solution)/shard_map/pallas_call | solution.py:840
